TPU v7x, 32 devices: a whole 2x2x4 slice. The times are simulated.
32 devices in a mesh: ka: 16 (over z, y, core), aux: 2 (over x).
Axes of the slice: x: 2, y: 2, z: 4, core: 2. Of those that a mesh axis runs over, the one named last changes fastest.
Arguments:
- coefficients: bfloat16 [16, 4096, 128], P('ka'), may hold values from -2.09375 to 2.09375
- triple: bfloat16 [64, 2, 64, 768], P('aux'), may hold values from -0.5 to 0.5
- neighbors: int32 [64, 2], P('aux'), may hold values from 0 to 63
- w_screened: bfloat16 [16, 768, 1536], P('ka', 'aux'), as said below
- partner: int32 [2, 16], replicated, may hold values from 0 to 15, each once within a row
- q_ids: int32 [2], replicated, may hold values from 0 to 15
Outputs:
- sigma: float32 [16, 64, 128], P('ka', 'aux')
Inputs may be any that keep to these rules, and one draw needn't show every extreme that they name: Each stored w_screened is Hermitian: its real block is symmetric and its imaginary block antisymmetric.
All inputs are finite; a program needn't handle non-finite values.
Results may differ from a plain program's by a relative error of at most 0.0085.
Values may be sent and summed in bfloat16 or wider, within the bound.
A program may use at most 128 MiB of HBM per device.

v0:
```python
import math

import jax
import jax.numpy as jnp
from jax import lax
from jax.sharding import PartitionSpec as P

CELL_ATOMS = 64
ORBITALS_PER_ATOM = 64
AUX_ATOM = 12
OCCUPIED_BANDS = 16
TRANSFERS = 2
NAUX = 768


def from_root(block, axis, source):
    block = jnp.where(lax.axis_index(axis) == source, block, jnp.zeros_like(block))
    return lax.psum(block, axis)


def from_partner(value, axis, distance):
    mask = 2**distance
    pairs = [(source, source ^ mask) for source in range(lax.axis_size(axis))]
    return lax.ppermute(value, axis, pairs)


def rotated_parts(values, band_count):
    return jnp.concatenate([-values[..., band_count:], values[..., :band_count]], axis=-1)


def apply_block(weights, start, values, band_count):
    kpoints, rows, occupied, doubled = values.shape
    real_cols = lax.dynamic_slice_in_dim(weights, start, rows, 1)
    imag_cols = lax.dynamic_slice_in_dim(weights, NAUX + start, rows, 1)
    flat = values.reshape(kpoints, rows, occupied * doubled)
    turned = rotated_parts(values, band_count).reshape(kpoints, rows, occupied * doubled)
    result = jnp.einsum("ab,kbx->kax", real_cols, flat, preferred_element_type=jnp.float32)
    result = result + jnp.einsum(
        "ab,kbx->kax", imag_cols, turned, preferred_element_type=jnp.float32
    )
    return result.reshape(kpoints, weights.shape[0], occupied, doubled)


def pair_blocks(left_values, right_values):
    kpoints = left_values.shape[0]
    doubled = left_values.shape[-1]
    left_flat = left_values.reshape(kpoints, -1, doubled)
    right_flat = right_values.reshape(kpoints, -1, doubled)
    return jnp.einsum("kxm,kxn->kmn", left_flat, right_flat, preferred_element_type=jnp.float32)


def sigma_parts(blocks, band_count):
    sigma_real = blocks[:, :band_count, :band_count] + blocks[:, band_count:, band_count:]
    sigma_imag = blocks[:, :band_count, band_count:] - blocks[:, band_count:, :band_count]
    return (sigma_real, sigma_imag)


def local(coefficients, triple, neighbors, w_screened, partner, q_ids):
    kpoints, orbitals, doubled = coefficients.shape
    band_count = doubled // 2
    local_atoms = triple.shape[0]
    local_aux = local_atoms * AUX_ATOM
    half_index = lax.axis_index("aux")
    prefactor = -1.0 / math.sqrt(TRANSFERS * NAUX * OCCUPIED_BANDS)
    screens = [
        from_root(w_screened[0], "ka", q_ids[momentum_transfer])
        for momentum_transfer in range(TRANSFERS)
    ]
    far_cols = jnp.concatenate(
        [
            coefficients[:, :, :OCCUPIED_BANDS],
            coefficients[:, :, band_count : band_count + OCCUPIED_BANDS],
        ],
        axis=2,
    )
    packed = far_cols.reshape(kpoints, orbitals * 2 * OCCUPIED_BANDS // 128, 128)
    spread = lax.all_to_all(packed, "ka", split_axis=1, concat_axis=0, tiled=True)
    permuted = jnp.take(spread, partner, axis=0)
    arrived = jnp.stack(
        [
            lax.all_to_all(
                permuted[momentum_transfer], "ka", split_axis=0, concat_axis=1, tiled=True
            )
            for momentum_transfer in range(TRANSFERS)
        ]
    )
    distant_coefficients = arrived.reshape(
        TRANSFERS, kpoints, CELL_ATOMS, ORBITALS_PER_ATOM, 2 * OCCUPIED_BANDS
    )
    own_rows = lax.dynamic_slice_in_dim(
        coefficients,
        half_index * local_atoms * ORBITALS_PER_ATOM,
        local_atoms * ORBITALS_PER_ATOM,
        1,
    )
    home_coefficients = own_rows.reshape(kpoints, local_atoms, ORBITALS_PER_ATOM, doubled)
    neighbour_coef = jnp.take(distant_coefficients, neighbors, axis=2)
    pair_half = jnp.einsum(
        "tkcjoy,cjox->tkcyx", neighbour_coef, triple, preferred_element_type=jnp.float32
    ).astype(jnp.bfloat16)
    pair_half = pair_half.reshape(
        TRANSFERS, kpoints, local_atoms, 2 * OCCUPIED_BANDS, AUX_ATOM, ORBITALS_PER_ATOM
    )
    combos = jnp.einsum(
        "kcix,tkcyai->tkcayx", home_coefficients, pair_half, preferred_element_type=jnp.float32
    )
    real_part = (
        combos[..., :OCCUPIED_BANDS, :band_count] + combos[..., OCCUPIED_BANDS:, band_count:]
    )
    imag_part = (
        combos[..., OCCUPIED_BANDS:, :band_count] - combos[..., :OCCUPIED_BANDS, band_count:]
    )
    products = jnp.concatenate([real_part, imag_part], axis=-1).astype(jnp.bfloat16)
    products = products.reshape(TRANSFERS, kpoints, local_aux, OCCUPIED_BANDS, doubled)
    pairs = products.reshape(TRANSFERS // 2, 2, kpoints, local_aux, OCCUPIED_BANDS, doubled)
    screen_pairs = jnp.stack(screens).reshape(TRANSFERS // 2, 2, local_aux, 2 * NAUX)
    outgoing = lax.dynamic_index_in_dim(pairs, 1 - half_index, 1, keepdims=False)
    incoming = from_partner(outgoing, "aux", 0)
    own_start = half_index * local_aux
    other_start = (1 - half_index) * local_aux
    full_weights = lax.dynamic_index_in_dim(screen_pairs[0], half_index, 0, keepdims=False)
    part_weights = lax.dynamic_index_in_dim(screen_pairs[0], 1 - half_index, 0, keepdims=False)
    full_values = lax.dynamic_index_in_dim(pairs[0], half_index, 0, keepdims=False)
    part_values = lax.dynamic_index_in_dim(pairs[0], 1 - half_index, 0, keepdims=False)
    cross = apply_block(full_weights, other_start, incoming[0], band_count)
    full_screened = (apply_block(full_weights, own_start, full_values, band_count) + cross).astype(
        jnp.bfloat16
    )
    part_screened = apply_block(part_weights, own_start, part_values, band_count).astype(
        jnp.bfloat16
    )
    cross_screened = cross.astype(jnp.bfloat16)
    diagonal = pair_blocks(full_values, full_screened) + pair_blocks(part_values, part_screened)
    diag_real, diag_imag = sigma_parts(diagonal, band_count)
    cross_real, cross_imag = sigma_parts(pair_blocks(full_values, cross_screened), band_count)
    total_real = diag_real + jnp.transpose(cross_real, (0, 2, 1))
    total_imag = diag_imag - jnp.transpose(cross_imag, (0, 2, 1))
    local_sigma = jnp.concatenate([total_real, total_imag], axis=-1)
    local_sigma = prefactor * local_sigma
    return lax.psum_scatter(
        local_sigma.astype(jnp.bfloat16), "aux", scatter_dimension=1, tiled=True
    ).astype(jnp.float32)


def solution(mesh):
    in_specs = (
        P("ka", None, None),
        P("aux", None, None, None),
        P("aux", None),
        P("ka", "aux", None),
        P(),
        P(),
    )
    out_specs = P("ka", "aux", None)
    return jax.shard_map(local, mesh=mesh, in_specs=in_specs, out_specs=out_specs, check_vma=False)
```

profile of v0, /device:TPU:0, one launch (start us, length us, event | category | flops | bytes accessed | tf_op | source)
XLA Modules:
  0.0 210.7 jit_solution(5651449956877544662)
XLA Ops:
  6.5 2.1 fusion.62
  10.9 2.2 %reduce = bf16[1024,128]{1,0:T(8,128)(2,1)S(1)} reduce(bf16[1024,1,128]{2,1,0:T(2,128)(2,1)S(1)} %bitcast.159, bf16[]{:T(256)} %broadcast.52), dimensions={1}, to_apply=%bitcast.134.reduce_sub_computation | reduce | bytes 524290
  13.1 0.8 reshape.297
  13.9 7.4 %all-to-all-start = ((bf16[16,2,4096]{2,1,0:T(2,128)(2,1)}), bf16[16,2,4096]{2,1,0:T(2,128)(2,1)S(1)}, u32[]{:S(2)}, u32[]{:S(2)}) async-start(bf16[16,2,4096]{2,1,0:T(2,128)(2,1)} %reshape.297), calls=%async_computation | async-start | bytes 524288 | tf_op jit(solution)/shard_map/all_to_all | solution.py:77
  23.3 8.0 %all-to-all-done = bf16[16,2,4096]{2,1,0:T(2,128)(2,1)S(1)} async-done(((bf16[16,2,4096]{2,1,0:T(2,128)(2,1)}), bf16[16,2,4096]{2,1,0:T(2,128)(2,1)S(1)}, u32[]{:S(2)}, u32[]{:S(2)}) %all-to-all-start) | async-done | bytes 262176 | tf_op jit(solution)/shard_map/all_to_all | solution.py:77
  32.4 0.8 slice_bitcast_fusion.1
  33.3 3.5 %all-to-all-start.1 = ((bf16[16,64,128]{2,1,0:T(8,128)(2,1)}), bf16[16,64,128]{2,1,0:T(8,128)(2,1)S(1)}, u32[]{:S(2)}, u32[]{:S(2)}) async-start(bf16[16,64,128]{2,1,0:T(8,128)(2,1)} %get-tuple-element.21), calls=%async_computation.1 | async-start | bytes 524288 | tf_op jit(solution)/shard_map/all_to_all | solution.py:81
  36.9 1.6 broadcast_select_fusion
  39.3 7.4 %all-to-all-done.1 = bf16[16,64,128]{2,1,0:T(8,128)(2,1)S(1)} async-done(((bf16[16,64,128]{2,1,0:T(8,128)(2,1)}), bf16[16,64,128]{2,1,0:T(8,128)(2,1)S(1)}, u32[]{:S(2)}, u32[]{:S(2)}) %all-to-all-start.1) | async-done | bytes 262176 | tf_op jit(solution)/shard_map/all_to_all | solution.py:81
  46.8 3.5 %all-to-all-start.2 = ((bf16[16,64,128]{2,1,0:T(8,128)(2,1)}), bf16[16,64,128]{2,1,0:T(8,128)(2,1)S(1)}, u32[]{:S(2)}, u32[]{:S(2)}) async-start(bf16[16,64,128]{2,1,0:T(8,128)(2,1)} %get-tuple-element.22), calls=%async_computation.2 | async-start | bytes 524288 | tf_op jit(solution)/shard_map/all_to_all | solution.py:81
  50.7 0.8 constant_dynamic-slice_fusion
  52.0 11.2 %all-to-all-done.2 = bf16[16,64,128]{2,1,0:T(8,128)(2,1)S(1)} async-done(((bf16[16,64,128]{2,1,0:T(8,128)(2,1)}), bf16[16,64,128]{2,1,0:T(8,128)(2,1)S(1)}, u32[]{:S(2)}, u32[]{:S(2)}) %all-to-all-start.2) | async-done | bytes 262176 | tf_op jit(solution)/shard_map/all_to_all | solution.py:81
  63.1 1.4 stack.19
  64.5 1.7 maximum_bitcast_fusion
  66.2 2.1 %gather_fusion.1 = bf16[64,2,64,32]{3,2,1,0:T(8,128)(2,1)} fusion(bf16[2,64,64,32]{3,2,1,0:T(8,128)(2,1)S(1)} %maximum_bitcast_fusion, s32[1024]{0:T(1024)S(1)} %pad_clamp_fusion), kind=kCustom, calls=%fused_computation.1 | custom fusion | bytes 1048832 | tf_op jit(solution)/shard_map/jit(_take)/gather | solution.py:97
  68.4 2.8 %copy.46 = bf16[64,2,64,32]{2,3,1,0:T(8,128)(2,1)} copy(bf16[64,2,64,32]{3,2,1,0:T(8,128)(2,1)} %gather_fusion.1) | data formatting | bytes 1048576 | tf_op jit(solution)/shard_map/jit(_take)/gather | solution.py:97
  71.1 4.9 %fusion.9 = bf16[2,1,32,32,768]{4,3,0,2,1:T(8,128)(2,1)S(1)} fusion(bf16[32,2,64,768]{3,2,1,0:T(8,128)(2,1)} %param.7, bf16[32,2,2,64,32]{3,4,2,1,0:T(8,128)(2,1)} %bitcast.155, pred[32,2]{1,0:T(8,128)(4,1)S(1)} %copy.40), kind=kOutput, calls=%fused_computation.12 | convolution fusion | flops 404488192 | bytes 9961536 | tf_op jit(solution)/shard_map/tkcjoy,cjox->tkcyx/dot_general | solution.py:98
  76.0 7.2 %reshape.296 = bf16[2,32,32,12,64]{4,3,2,0,1:T(8,128)(2,1)} reshape(bf16[2,1,32,32,768]{4,3,0,2,1:T(8,128)(2,1)S(1)} %fusion.9) | data formatting | bytes 6291456 | tf_op jit(solution)/shard_map/reshape.12
  83.2 5.1 %fusion.6 = f32[2,1,32,12,32,128]{5,4,3,0,2,1:T(8,128)S(1)} fusion(bf16[32,64,128,1,1]{2,1,4,3,0:T(8,128)(2,1)} %bitcast.160, bf16[2,32,32,12,64]{4,3,2,0,1:T(8,128)(2,1)} %reshape.296), kind=kOutput, calls=%fused_computation.11 | convolution fusion | flops 402653184 | bytes 16252928 | tf_op jit(solution)/shard_map/kcix,tkcyai->tkcayx/dot_general | solution.py:104
  88.3 3.7 %fusion = (bf16[2,1,32,12,16,64]{5,4,3,0,2,1:T(8,128)(2,1)S(1)}, bf16[2,1,32,12,16,64]{5,4,3,0,2,1:T(8,128)(2,1)S(1)}) fusion(f32[2,1,32,12,32,128]{5,4,3,0,2,1:T(8,128)S(1)} %fusion.6), kind=kLoop, calls=%fused_computation.3 | loop fusion | flops 3145728 | bytes 15728640 | tf_op jit(solution)/shard_map/convert.6
  93.3 2.1 fusion.17
  95.4 1.6 collective-permute-start
  97.0 1.7 fusion.14
  99.3 2.0 pad_maximum_fusion.2
  102.0 2.1 %pad_maximum_fusion = bf16[1,384,16,128]{3,2,1,0:T(8,128)(2,1)} fusion(bf16[1,384,16,64]{3,2,1,0:T(8,128)(2,1)S(1)} %get-tuple-element.14, bf16[1,384,16,64]{3,2,1,0:T(8,128)(2,1)S(1)} %get-tuple-element.13), kind=kLoop, calls=%fused_computation.47 | loop fusion | flops 3145728 | bytes 3145728 | tf_op jit(solution)/shard_map/concatenate | solution.py:28
  104.1 42.1 %all-reduce.3.cloned.1.call-done = (bf16[1,384,1536]{2,1,0:T(8,128)(2,1)}, bf16[1,384,1536]{2,1,0:T(8,128)(2,1)}) async-done(((bf16[1,384,1536]{2,1,0:T(8,128)(2,1)}, bf16[1,384,1536]{2,1,0:T(8,128)(2,1)}), (bf16[1,384,1536]{2,1,0:T(8,128)(2,1)}, bf16[1,384,1536]{2,1,0:T(8,128)(2,1)})) %all-reduce.3.cloned.1.call-update) | async-done | bytes 2359312 | tf_op jit(solution)/shard_map/psum | solution.py:18
  146.2 1.4 constant_dynamic-update-slice_fusion.1
  148.0 1.3 fusion.20
  149.3 0.9 copy-done.4
  150.2 2.5 %fusion.11 = bf16[1,384,2048]{1,2,0:T(8,128)(2,1)} fusion(f32[2048,384]{1,0:T(8,128)S(1)} %fusion.20, bf16[48,8,16,128]{3,2,1,0:T(8,128)(2,1)S(1)} %bitcast.157, bf16[2,384,1536]{2,1,0:T(8,128)(2,1)S(1)} %constant_dynamic-update-slice_fusion, s32[]{:T(128)S(6)} %select_n.104, s32[]{:T(128)S(6)} %select_n.98), kind=kOutput, calls=%fused_computation.23 | convolution fusion | flops 605552640 | bytes 6586376 | tf_op jit(solution)/shard_map/ab,kbx->kax/dot_general | solution.py:38
  152.7 2.6 %copy.55 = bf16[1,384,2048]{2,1,0:T(8,128)(2,1)} copy(bf16[1,384,2048]{1,2,0:T(8,128)(2,1)} %fusion.11) | data formatting | bytes 3145728 | tf_op jit(solution)/shard_map/convert_element_type | solution.py:129
  155.3 3.7 %convert_element_type.101 = bf16[6144,128]{1,0:T(8,128)(2,1)} reshape(bf16[1,384,2048]{2,1,0:T(8,128)(2,1)} %copy.55) | data formatting | bytes 3145728 | tf_op jit(solution)/shard_map/convert_element_type | solution.py:129
  159.1 2.3 %fusion.30 = f32[2048,384]{1,0:T(8,128)S(1)} fusion(bf16[48,8,16,128]{3,2,1,0:T(8,128)(2,1)S(1)} %bitcast.144, bf16[2,384,1536]{2,1,0:T(8,128)(2,1)} %copy-done.5, s32[]{:T(128)S(6)} %select_n.94, s32[]{:T(128)S(6)} %select_n.96), kind=kOutput, calls=%fused_computation.41 | convolution fusion | flops 603979776 | bytes 5013512 | tf_op jit(solution)/shard_map/ab,kbx->kax/dot_general | solution.py:37
  161.3 2.6 %slice_negate_fusion.1 = (bf16[1,384,16,64]{3,2,1,0:T(8,128)(2,1)S(1)}, bf16[1,384,16,64]{3,2,1,0:T(8,128)(2,1)S(1)}) fusion(bf16[1,384,16,128]{3,2,1,0:T(8,128)(2,1)} %bitcast.31), kind=kLoop, calls=%fused_computation.45 | loop fusion | flops 393216 | bytes 3145728 | tf_op jit(solution)/shard_map/neg | solution.py:28
  163.9 0.9 pad_maximum_fusion.1
  164.8 2.2 %fusion.23 = f32[2048,384]{1,0:T(8,128)S(1)} fusion(bf16[48,8,16,128]{3,2,1,0:T(8,128)(2,1)S(1)} %bitcast.154, bf16[2,384,1536]{2,1,0:T(8,128)(2,1)} %copy-done.5, s32[]{:T(128)S(6)} %select_n.94, s32[]{:T(128)S(6)} %select_n.103), kind=kOutput, calls=%fused_computation.34 | convolution fusion | flops 603979776 | bytes 5013512 | tf_op jit(solution)/shard_map/ab,kbx->kax/dot_general | solution.py:38
  167.0 2.8 %convolution_add_fusion = f32[2048,384]{1,0:T(8,128)S(1)} fusion(f32[2048,384]{1,0:T(8,128)S(1)} %fusion.23, bf16[48,8,16,128]{3,2,1,0:T(8,128)(2,1)} %bitcast.70, bf16[2,384,1536]{2,1,0:T(8,128)(2,1)} %copy-done.5, s32[]{:T(128)S(6)} %select_n.94, s32[]{:T(128)S(6)} %select_n.101), kind=kOutput, calls=%fused_computation.17 | convolution fusion | flops 604766208 | bytes 8159240 | tf_op jit(solution)/shard_map/ab,kbx->kax/dot_general | solution.py:37
  169.8 1.3 convert_bitcast_fusion
  171.8 3.6 %fusion.10 = bf16[1,384,2048]{1,2,0:T(8,128)(2,1)} fusion(f32[2048,384]{1,0:T(8,128)S(1)} %convolution_add_fusion, f32[2048,384]{1,0:T(8,128)S(1)} %fusion.30, bf16[48,8,16,128]{3,2,1,0:T(8,128)(2,1)S(1)} %bitcast.156, bf16[2,384,1536]{2,1,0:T(8,128)(2,1)} %copy-done.5, s32[]{:T(128)S(6)} %select_n.94, s32[]{:T(128)S(6)} %select_n.98), kind=kOutput, calls=%fused_computation.22 | convolution fusion | flops 606339072 | bytes 9732104 | tf_op jit(solution)/shard_map/ab,kbx->kax/dot_general | solution.py:38
  175.4 2.7 %copy.54 = bf16[1,384,2048]{2,1,0:T(8,128)(2,1)} copy(bf16[1,384,2048]{1,2,0:T(8,128)(2,1)} %fusion.10) | data formatting | bytes 3145728 | tf_op jit(solution)/shard_map/convert_element_type | solution.py:126
  178.1 3.7 %convert_element_type.97 = bf16[6144,128]{1,0:T(8,128)(2,1)} reshape(bf16[1,384,2048]{2,1,0:T(8,128)(2,1)} %copy.54) | data formatting | bytes 3145728 | tf_op jit(solution)/shard_map/convert_element_type | solution.py:126
  181.8 2.6 %copy.56 = bf16[1,384,2048]{2,1,0:T(8,128)(2,1)} copy(bf16[1,384,2048]{1,2,0:T(8,128)(2,1)} %convert_bitcast_fusion) | data formatting | bytes 3145728 | tf_op jit(solution)/shard_map/convert_element_type | solution.py:132
  184.4 3.7 %convert_element_type.105 = bf16[6144,128]{1,0:T(8,128)(2,1)} reshape(bf16[1,384,2048]{2,1,0:T(8,128)(2,1)} %copy.56) | data formatting | bytes 3145728 | tf_op jit(solution)/shard_map/convert_element_type | solution.py:132
  188.2 2.1 %fusion.64 = f32[128,128]{1,0:T(8,128)S(1)} fusion(bf16[6144,128]{1,0:T(8,128)(2,1)S(1)} %bitcast.145, bf16[6144,128]{1,0:T(8,128)(2,1)} %convert_element_type.97), kind=kOutput, calls=%fused_computation.104 | convolution fusion | flops 201326592 | bytes 3211264 | tf_op jit(solution)/shard_map/kxm,kxn->kmn/dot_general | solution.py:49
  191.0 0.8 copy-done.2
  192.5 0.7 fusion.54
  193.2 9.4 %reduce-scatter.2.cloned.1.call-done = bf16[1,32,128]{2,1,0:T(8,128)(2,1)} async-done(((bf16[1,64,128]{2,1,0:T(8,128)(2,1)}), bf16[1,32,128]{2,1,0:T(8,128)(2,1)}) %reduce-scatter.2.cloned.1.call-update) | async-done | bytes 8208 | tf_op jit(solution)/shard_map/reduce_scatter | solution.py:140
  202.6 1.3 convert_element_type.107
  (55 shorter events, 10.6 us)
Async XLA Ops:
  9.7 11.6 %copy-start.9 = (s32[2,16]{1,0:T(2,128)S(1)}, s32[2,16]{1,0:T(2,128)}, u32[]{:S(2)}) copy-start(s32[2,16]{1,0:T(2,128)} %param.10) | copy-start | bytes 388
  9.8 11.7 %copy-start.8 = (s32[2]{0:T(128)S(1)}, s32[2]{0:T(128)}, u32[]{:S(2)}) copy-start(s32[2]{0:T(128)} %param.11) | copy-start | bytes 28
  13.9 17.4 %all-to-all-start = ((bf16[16,2,4096]{2,1,0:T(2,128)(2,1)}), bf16[16,2,4096]{2,1,0:T(2,128)(2,1)S(1)}, u32[]{:S(2)}, u32[]{:S(2)}) async-start(bf16[16,2,4096]{2,1,0:T(2,128)(2,1)} %reshape.297), calls=%async_computation | async-start | bytes 524288 | tf_op jit(solution)/shard_map/all_to_all | solution.py:77
  32.3 4.6 %copy-start.7 = (bf16[1,384,1536]{2,1,0:T(8,128)(2,1)S(1)}, bf16[1,384,1536]{2,1,0:T(8,128)(2,1)}, u32[]{:S(2)}) copy-start(bf16[1,384,1536]{2,1,0:T(8,128)(2,1)} %param.9) | copy-start | bytes 3538948
  33.3 13.5 %all-to-all-start.1 = ((bf16[16,64,128]{2,1,0:T(8,128)(2,1)}), bf16[16,64,128]{2,1,0:T(8,128)(2,1)S(1)}, u32[]{:S(2)}, u32[]{:S(2)}) async-start(bf16[16,64,128]{2,1,0:T(8,128)(2,1)} %get-tuple-element.21), calls=%async_computation.1 | async-start | bytes 524288 | tf_op jit(solution)/shard_map/all_to_all | solution.py:81
  36.8 109.4 %all-reduce.3.cloned.1.call-start = ((), (), s32[]{:S(2)}) async-start(), calls=%async_computation.5 | async-start | bytes 4718592 | tf_op jit(solution)/shard_map/psum | solution.py:18
  38.5 0.7 copy-start.10
  38.5 12.2 %copy-start = (bf16[1,4096,128]{2,1,0:T(8,128)(2,1)S(1)}, bf16[1,4096,128]{2,1,0:T(8,128)(2,1)}, u32[]{:S(2)}) copy-start(bf16[1,4096,128]{2,1,0:T(8,128)(2,1)} %param.6) | copy-start | bytes 3145732
  46.8 16.4 %all-to-all-start.2 = ((bf16[16,64,128]{2,1,0:T(8,128)(2,1)}), bf16[16,64,128]{2,1,0:T(8,128)(2,1)S(1)}, u32[]{:S(2)}, u32[]{:S(2)}) async-start(bf16[16,64,128]{2,1,0:T(8,128)(2,1)} %get-tuple-element.22), calls=%async_computation.2 | async-start | bytes 524288 | tf_op jit(solution)/shard_map/all_to_all | solution.py:81
  50.3 152.2 %reduce-scatter.2.cloned.1.call-start = ((), (), s32[]{:S(2)}) async-start(), calls=%async_computation.4 | async-start | bytes 24576 | tf_op jit(solution)/shard_map/reduce_scatter | solution.py:140
  95.4 65.9 %collective-permute-start = (bf16[1,1,384,16,128]{4,3,2,1,0:T(8,128)(2,1)}, bf16[1,1,384,16,128]{4,3,2,1,0:T(8,128)(2,1)}, u32[]{:S(2)}, u32[]{:S(2)}) collective-permute-start(bf16[1,1,384,16,128]{4,3,2,1,0:T(8,128)(2,1)} %fusion.17), channel_id=1, source_target_pairs={{0,1},{1,0},{2,3},{3,2},{4,5},{5,4},{6,7},{7,6},{8,9},{9,8},{10,11... | collective-permute-start | bytes 4718600 | tf_op jit(solution)/shard_map/ppermute | solution.py:24
  146.2 1.6 copy-start.6
  147.9 1.4 copy-start.5
  147.9 2.3 %copy-start.4 = (bf16[1,384,16,128]{3,2,1,0:T(8,128)(2,1)S(1)}, bf16[1,384,16,128]{3,2,1,0:T(8,128)(2,1)}, u32[]{:S(2)}) copy-start(bf16[1,384,16,128]{3,2,1,0:T(8,128)(2,1)} %pad_maximum_fusion.2) | copy-start | bytes 4718596
  169.8 2.0 copy-start.1
  188.2 2.1 %copy-start.3 = (bf16[6144,128]{1,0:T(8,128)(2,1)S(1)}, bf16[6144,128]{1,0:T(8,128)(2,1)}, u32[]{:S(2)}) copy-start(bf16[6144,128]{1,0:T(8,128)(2,1)} %convert_element_type.105) | copy-start | bytes 4718596
  190.3 1.4 copy-start.2
Sparse Core Ops, SparseCore 0:
  41.2 104.9 all-reduce.2
  193.3 9.2 reduce-scatter.1
where the time goes:
time: 212 us; the launch traced here: 211 us
  waiting for transfers between devices  78.2 us (37%)
  local copies, waits for them, and re-layouts  47.6 us (22%)
  matrix products  28.1 us (13%)
  other arithmetic  25.5 us (12%)
  starting transfers between devices  16.3 us (8%)
  between operations  15.1 us (7%)
    psum x1, waiting for transfers between devices, from_root(): return lax.psum(block, axis)  42.1 us
    all_to_all x2, waiting for transfers between devices, local(): lax.all_to_all(permuted[momentum_transfer], 'ka', split_axis=0, concat_ax...  18.6 us
    reduce_scatter x1, waiting for transfers between devices, local(): lax.psum_scatter(local_sigma.astype(jnp.bfloat16), 'aux', scatter_dimensi...  9.4 us
    another operation x3, local copies, waits for them, and re-layouts  8.42 us
    dot_general x3, matrix products, apply_block(): jnp.einsum('ab,kbx->kax', imag_cols, turned, preferred_element_type=jnp.f...  8.36 us
    all_to_all x1, waiting for transfers between devices, local(): lax.all_to_all(packed, 'ka', split_axis=1, concat_axis=0, tiled=True)  8.01 us
    all_to_all x1, starting transfers between devices, local(): lax.all_to_all(packed, 'ka', split_axis=1, concat_axis=0, tiled=True)  7.41 us
    all_to_all x2, starting transfers between devices, local(): lax.all_to_all(permuted[momentum_transfer], 'ka', split_axis=0, concat_ax...  7.06 us
  transfers between devices with their start and end apart: 6, of which 5 were waited for; matrix products, arithmetic and copies ran while one was open for 27% of the time, Pallas kernels for 0%

commit v1 on v0

v1 whole, which is shorter than its diff:
```python
import functools
import math

import jax
import jax.numpy as jnp
from jax import lax
from jax.experimental import pallas as pl
from jax.experimental.pallas import tpu as pltpu
from jax.sharding import PartitionSpec as P

AUX_ATOM = 12
OCC = 16
VMEM = pltpu.VMEM
SMEM = pltpu.SMEM


def bounce_kernel(n, transfers, partner_ref, src_ref, out_ref, spread, picked, s1, r1, s2, r2):
    me = lax.axis_index("ka")
    barrier = pltpu.get_barrier_semaphore()

    def greet(off, carry):
        dst = lax.rem(me + off, n)
        pl.semaphore_signal(
            barrier, inc=1, device_id={"ka": dst}, device_id_type=pl.DeviceIdType.MESH
        )
        return carry

    lax.fori_loop(1, n, greet, 0)
    pl.semaphore_wait(barrier, n - 1)

    def first(off):
        dst = lax.rem(me + off, n)
        return pltpu.make_async_remote_copy(
            src_ref=src_ref.at[dst],
            dst_ref=spread.at[me],
            send_sem=s1.at[off],
            recv_sem=r1.at[off],
            device_id={"ka": dst},
            device_id_type=pl.DeviceIdType.MESH,
        )

    def second(t, off):
        dst = lax.rem(me + off, n)
        return pltpu.make_async_remote_copy(
            src_ref=picked.at[t, dst],
            dst_ref=out_ref.at[t, me],
            send_sem=s2.at[t, off],
            recv_sem=r2.at[t, off],
            device_id={"ka": dst},
            device_id_type=pl.DeviceIdType.MESH,
        )

    def start_first(off, carry):
        first(off).start()
        return carry

    def wait_first(off, carry):
        first(off).wait()
        return carry

    lax.fori_loop(1, n, start_first, 0)
    spread[me] = src_ref[me]
    lax.fori_loop(1, n, wait_first, 0)
    for t in range(transfers):

        def pick(k, carry, t=t):
            picked[t, k] = spread[partner_ref[t, k]]
            return carry

        def start_second(off, carry, t=t):
            second(t, off).start()
            return carry

        lax.fori_loop(0, n, pick, 0)
        lax.fori_loop(1, n, start_second, 0)
        out_ref[t, me] = picked[t, me]
    for t in range(transfers):

        def wait_second(off, carry, t=t):
            second(t, off).wait()
            return carry

        lax.fori_loop(1, n, wait_second, 0)


def bounce(src, partner, transfers):
    n, rows, lanes = src.shape
    return pl.pallas_call(
        functools.partial(bounce_kernel, n, transfers),
        out_shape=jax.ShapeDtypeStruct((transfers, n, rows, lanes), src.dtype),
        in_specs=[pl.BlockSpec(memory_space=SMEM), pl.BlockSpec(memory_space=VMEM)],
        out_specs=pl.BlockSpec(memory_space=VMEM),
        scratch_shapes=[
            VMEM((n, rows, lanes), src.dtype),
            VMEM((transfers, n, rows, lanes), src.dtype),
            pltpu.SemaphoreType.DMA((n,)),
            pltpu.SemaphoreType.DMA((n,)),
            pltpu.SemaphoreType.DMA((transfers, n)),
            pltpu.SemaphoreType.DMA((transfers, n)),
        ],
        compiler_params=pltpu.CompilerParams(collective_id=0, has_side_effects=True),
        name="bounce",
    )(partner, src)


def far_kernel(coef_ref, out_ref):
    for p in range(out_ref.shape[0]):
        block = coef_ref[p * 128 : (p + 1) * 128, :].astype(jnp.float32).T
        half = block.shape[0] // 2
        out_ref[p, 0:OCC] = block[0:OCC].astype(jnp.bfloat16)
        out_ref[p, OCC : 2 * OCC] = block[half : half + OCC].astype(jnp.bfloat16)


def far_pairs(coef):
    orbitals, doubled = coef.shape
    per = 4
    return pl.pallas_call(
        far_kernel,
        grid=(orbitals // 128 // per,),
        out_shape=jax.ShapeDtypeStruct((orbitals // 128, 2 * OCC, 128), jnp.bfloat16),
        in_specs=[pl.BlockSpec((per * 128, doubled), lambda g: (g, 0))],
        out_specs=pl.BlockSpec((per, 2 * OCC, 128), lambda g: (g, 0, 0)),
        name="far_pairs",
    )(coef)


def pair_kernel(group, nb_ref, half_ref, far_ref, triple_ref, coef_ref, own_ref, part_ref, stage):
    step = pl.program_id(0)
    low = lax.broadcasted_iota(jnp.int32, (4 * OCC, 128), 1) < 64
    sign = jnp.where(lax.broadcasted_iota(jnp.int32, (64, 128), 1) < 64, 1.0, -1.0)
    zero = jnp.zeros((64, 128), jnp.bfloat16)
    for g in range(group):
        c = step * group + g
        n0 = nb_ref[c, 0]
        n1 = nb_ref[c, 1]
        x0 = far_ref[n0 % 2, n0 // 2]
        x1 = far_ref[1 - n1 % 2, n1 // 2]
        lhs = jnp.where(low, x0, x1)
        half = jnp.dot(lhs, triple_ref[g], preferred_element_type=jnp.float32)
        half = half.astype(jnp.bfloat16)
        top, bottom = half[: 2 * OCC], half[2 * OCC :]
        home = coef_ref[g].astype(jnp.float32)
        with_real = (home * sign).astype(jnp.bfloat16)
        with_imag = pltpu.roll(home, 64, 1).astype(jnp.bfloat16)
        rhs = jnp.concatenate(
            [
                jnp.concatenate([with_real, zero], axis=1),
                jnp.concatenate([zero, with_real], axis=1),
                jnp.concatenate([with_imag, zero], axis=1),
                jnp.concatenate([zero, with_imag], axis=1),
            ],
            axis=0,
        )
        rows = jnp.concatenate(
            [
                jnp.concatenate(
                    [top[:, s * 128 : (s + 1) * 128], bottom[:, s * 128 : (s + 1) * 128]], axis=1
                )
                for s in range(AUX_ATOM // 2)
            ],
            axis=0,
        )
        prod = jnp.dot(rows, rhs, preferred_element_type=jnp.float32)
        for s in range(AUX_ATOM // 2):
            for t in range(2):
                for b in range(2):
                    at = (g * AUX_ATOM + 2 * s + b) * OCC
                    r = s * 2 * OCC + t * OCC
                    stage[t, at : at + OCC, :] = prod[r : r + OCC, b * 128 : (b + 1) * 128]
    count = group * AUX_ATOM
    for t, out in enumerate((own_ref, part_ref)):
        for l in range(OCC):
            out[l] = stage[t, pl.ds(l, count, stride=OCC), :].astype(jnp.bfloat16)


def pair_products(far, triple, coef, neighbors, half):
    atoms = triple.shape[0]
    group = 4
    shape = jax.ShapeDtypeStruct((OCC, atoms * AUX_ATOM, 128), jnp.bfloat16)
    steps = atoms // group
    out_spec = pl.BlockSpec((OCC, group * AUX_ATOM, 128), lambda c, nb, h: (0, c, 0))
    return pl.pallas_call(
        functools.partial(pair_kernel, group),
        grid_spec=pltpu.PrefetchScalarGridSpec(
            num_scalar_prefetch=2,
            grid=(steps,),
            in_specs=[
                pl.BlockSpec(far.shape, lambda c, nb, h: (0, 0, 0, 0)),
                pl.BlockSpec((group,) + triple.shape[1:], lambda c, nb, h: (c, 0, 0)),
                pl.BlockSpec((group,) + coef.shape[1:], lambda c, nb, h: (h[0] * steps + c, 0, 0)),
            ],
            out_specs=[out_spec, out_spec],
            scratch_shapes=[VMEM((2, group * AUX_ATOM * OCC, 128), jnp.float32)],
        ),
        out_shape=[shape, shape],
        cost_estimate=pl.CostEstimate(
            flops=1_600_000_000, bytes_accessed=30_000_000, transcendentals=0
        ),
        name="pair_products",
    )(neighbors, half, far, triple, coef)


def screen_kernel(count, *refs):
    w_ref = refs[0]
    out_ref = refs[-1]
    rows = w_ref.shape[1] // 2

    @pl.when(pl.program_id(0) == 0)
    def _():
        out_ref[...] = jnp.zeros_like(out_ref)

    sign = jnp.where(lax.broadcasted_iota(jnp.int32, (rows, 128), 1) < 64, -1.0, 1.0)
    total = out_ref[...]
    for u in range(count):
        right, left = refs[1 + 2 * u], refs[2 + 2 * u]
        wide = jnp.concatenate([right[0], right[1]], axis=1)
        prod = jnp.dot(w_ref[u], wide, preferred_element_type=jnp.float32)
        for e in range(2):
            re = prod[:rows, e * 128 : (e + 1) * 128]
            im = prod[rows:, e * 128 : (e + 1) * 128]
            scr = (re + sign * pltpu.roll(im, 64, 1)).astype(jnp.bfloat16)
            total = total + lax.dot_general(
                left[e], scr, (((0,), (0,)), ((), ())), preferred_element_type=jnp.float32
            )
    out_ref[...] = total


def screen(weights, pairs, name):
    count = weights.shape[0]
    occ, rows, doubled = pairs[0][0].shape
    spec = pl.BlockSpec((2, rows, doubled), lambda s: (s, 0, 0))
    return pl.pallas_call(
        functools.partial(screen_kernel, count),
        grid=(occ // 2,),
        out_shape=jax.ShapeDtypeStruct((doubled, doubled), jnp.float32),
        in_specs=[pl.BlockSpec(weights.shape, lambda s: (0, 0, 0))] + [spec] * (2 * count),
        out_specs=pl.BlockSpec((doubled, doubled), lambda s: (0, 0)),
        cost_estimate=pl.CostEstimate(
            flops=count * 4_000_000_000, bytes_accessed=count * 10_000_000, transcendentals=0
        ),
        name=name,
    )(weights, *[x for pair in pairs for x in pair])


def swap(value, axis, mask):
    pairs = [(source, source ^ mask) for source in range(lax.axis_size(axis))]
    return lax.ppermute(value, axis, pairs)


def spread_root(value, axis):
    n = lax.axis_size(axis)
    me = lax.axis_index(axis)
    rows, cols = value.shape
    bits = [1 << b for b in range(n.bit_length() - 1)]
    for bit in bits:
        mine = (me // bit) % 2
        halves = value.reshape(2, value.shape[0] // 2, cols)
        kept = lax.dynamic_index_in_dim(halves, mine, 0, keepdims=False)
        sent = lax.dynamic_index_in_dim(halves, 1 - mine, 0, keepdims=False)
        value = kept + swap(sent, axis, bit)
    for bit in reversed(bits):
        mine = (me // bit) % 2
        other = swap(value, axis, bit)
        value = jnp.concatenate(
            [jnp.where(mine == 0, value, other), jnp.where(mine == 0, other, value)], axis=0
        )
    return value


def local(coefficients, triple, neighbors, w_screened, partner, q_ids):
    transfers = partner.shape[0]
    coef = coefficients[0]
    orbitals, doubled = coef.shape
    bands = doubled // 2
    atoms, neigh, per_atom, width = triple.shape
    aux_rows = atoms * AUX_ATOM
    naux = w_screened.shape[2] // 2
    n = lax.axis_size("ka")
    me = lax.axis_index("ka")
    half = lax.axis_index("aux")
    prefactor = -1.0 / math.sqrt(transfers * naux * OCC)

    order = jnp.stack([half, 1 - half])
    partner_here = jnp.take(partner, order, axis=0)
    q_here = jnp.take(q_ids, order, axis=0)

    weights = w_screened[0].reshape(aux_rows, 2, 2, aux_rows)
    own = lax.dynamic_index_in_dim(weights, half, 2, keepdims=False)
    other = lax.dynamic_index_in_dim(weights, 1 - half, 2, keepdims=False)
    own = jnp.moveaxis(own, 1, 0) * jnp.bfloat16(0.5)
    other = jnp.moveaxis(other, 1, 0)
    zero = jnp.zeros_like(own)
    first = me == q_here[0]
    second = me == q_here[1]
    payload = jnp.concatenate(
        [
            jnp.where(first, own, zero),
            jnp.where(second, own, zero),
            jnp.where(first, other, zero),
        ],
        axis=0,
    ).reshape(6 * aux_rows, aux_rows)
    payload = spread_root(payload, "ka").reshape(3, 2 * aux_rows, aux_rows)

    packed = far_pairs(coef)
    rows = packed.shape[0] * packed.shape[1]
    arrived = bounce(packed.reshape(n, rows // n, 128), partner_here, transfers)
    far = arrived.reshape(transfers, packed.shape[0], 2, OCC, 128)
    far = jnp.transpose(far, (1, 2, 0, 3, 4)).reshape(packed.shape[0], 2 * transfers * OCC, 128)
    far = jnp.stack([far, jnp.concatenate([far[..., 64:], far[..., :64]], axis=-1)])

    mine, part = pair_products(
        far,
        triple.reshape(atoms, neigh * per_atom, width),
        coef.reshape(orbitals // per_atom, per_atom, doubled),
        neighbors,
        half.astype(jnp.int32).reshape(1),
    )
    incoming = swap(part, "aux", 1)
    blocks = screen(payload[:2], [(mine, mine), (part, part)], "screen_own")
    blocks = blocks + screen(payload[2:], [(incoming, mine)], "screen_cross")
    real = blocks[:bands, :bands] + blocks[bands:, bands:]
    imag = blocks[:bands, bands:] - blocks[bands:, :bands]
    sigma = prefactor * jnp.concatenate([real + real.T, imag - imag.T], axis=-1)
    halves = sigma.reshape(2, bands // 2, doubled)
    sent = lax.dynamic_index_in_dim(halves, 1 - half, 0, keepdims=False)
    kept = lax.dynamic_index_in_dim(halves, half, 0, keepdims=False)
    return (kept + swap(sent, "aux", 1))[None]


def solution(mesh):
    in_specs = (
        P("ka", None, None),
        P("aux", None, None, None),
        P("aux", None),
        P("ka", "aux", None),
        P(),
        P(),
    )
    out_specs = P("ka", "aux", None)
    return jax.shard_map(local, mesh=mesh, in_specs=in_specs, out_specs=out_specs, check_vma=False)
```

time: 212 us -> 150 us (0.71)
  Pallas kernels: 0 us -> 62.8 us
  local copies, waits for them, and re-layouts: 47.6 us -> 8.63 us
  matrix products: 28.1 us -> 0 us
  waiting for transfers between devices: 78.2 us -> 52 us
  other arithmetic: 25.5 us -> 6.46 us
  between operations: 15.1 us -> 1.47 us
    pallas_call x0 -> x5, Pallas kernels: none -> 62.8 us  [the longest x1 24.5 us: bounce(): pl.pallas_call(functools.partial(bounce_kernel, n, transfers), out_shape=...]
    ppermute x1 -> x10, waiting for transfers between devices: 0.01 us -> 52 us  [swap(): return lax.ppermute(value, axis, pairs)]
    psum x1 -> x0, waiting for transfers between devices: 42.1 us -> none  [from_root(): return lax.psum(block, axis)]
    dot_general x11 -> x0, matrix products: 28.1 us -> none  [the longest x3 8.36 us: apply_block(): jnp.einsum('ab,kbx->kax', imag_cols, turned, preferred_element_type=jnp.f...]
    all_to_all x3 -> x0, waiting for transfers between devices: 26.6 us -> none  [the longest x2 18.6 us: local(): lax.all_to_all(permuted[momentum_transfer], 'ka', split_axis=0, concat_ax...]
    convert_element_type x6 -> x0, local copies, waits for them, and re-layouts: 19.1 us -> none  [the longest x2 6.42 us: local(): (apply_block(full_weights, own_start, full_values, band_count) + cross).a...]
    ppermute x1 -> x10, starting transfers between devices: 1.56 us -> 17.4 us  [swap(): return lax.ppermute(value, axis, pairs)]
    all_to_all x3 -> x0, starting transfers between devices: 14.5 us -> none  [the longest x1 7.41 us: local(): lax.all_to_all(packed, 'ka', split_axis=1, concat_axis=0, tiled=True)]
  transfers between devices with their start and end apart: 6 -> 10, of which waited for: 5 -> 9; matrix products, arithmetic and copies ran while one was open for 27% -> 5% of each run, Pallas kernels for 0% -> 37%
where the time goes in v1:
time: 150 us; the launch traced here: 149 us
  Pallas kernels  62.8 us (42%)
  waiting for transfers between devices  52 us (35%)
  starting transfers between devices  17.4 us (12%)
  local copies, waits for them, and re-layouts  8.63 us (6%)
  other arithmetic  6.46 us (4%)
    ppermute x10, waiting for transfers between devices, swap(): return lax.ppermute(value, axis, pairs)  52 us
    pallas_call x1, Pallas kernels, bounce(): pl.pallas_call(functools.partial(bounce_kernel, n, transfers), out_shape=...  24.5 us
    pallas_call x2, Pallas kernels, screen(): pl.pallas_call(functools.partial(screen_kernel, count), grid=(occ // 2,),...  22.7 us
    ppermute x10, starting transfers between devices, swap(): return lax.ppermute(value, axis, pairs)  17.4 us
    pallas_call x1, Pallas kernels, pair_products(): pl.pallas_call(functools.partial(pair_kernel, group), grid_spec=pltpu.Pre...  10.3 us
    pallas_call x1, Pallas kernels, far_pairs(): pl.pallas_call(far_kernel, grid=(orbitals // 128 // per,), out_shape=jax....  5.28 us
  transfers between devices with their start and end apart: 10, of which 9 were waited for; matrix products, arithmetic and copies ran while one was open for 5% of the time, Pallas kernels for 37%

profile of v1, /device:TPU:0, one launch (start us, length us, event | category | flops | bytes accessed | tf_op | source)
XLA Modules:
  0.0 148.7 jit_solution(11901330986905971749)
XLA Ops:
  0.1 1.3 gather_fusion
  1.4 0.1 broadcast_select_fusion.9
  1.5 0.6 fusion.6
  3.4 1.7 %copy.18 = bf16[1,384,1536]{1,2,0:T(8,128)(2,1)S(1)} copy(bf16[1,384,1536]{2,1,0:T(8,128)(2,1)} %param.9) | data formatting | bytes 2359296 | tf_op args[3]
  5.1 0.1 fusion.2
  5.2 0.1 fusion.1
  5.3 0.2 pad_maximum_fusion
  5.6 1.1 copy.25
  6.7 0.1 dynamic-slice_bitcast_fusion
  6.8 0.6 collective-permute-start
  7.4 2.1 %collective-permute-done = bf16[1152,384]{1,0:T(8,128)(2,1)S(1)} collective-permute-done((bf16[1152,384]{1,0:T(8,128)(2,1)S(1)}, bf16[1152,384]{1,0:T(8,128)(2,1)S(1)}, u32[]{:S(2)}, u32[]{:S(2)}) %collective-permute-start) | collective-permute-done | bytes 884768 | tf_op jit(solution)/shard_map/ppermute | solution.py:247
  9.5 0.1 bitcast_add_fusion
  9.6 2.9 %collective-permute-start.1 = (bf16[576,384]{1,0:T(8,128)(2,1)S(1)}, bf16[576,384]{1,0:T(8,128)(2,1)S(1)}, u32[]{:S(2)}, u32[]{:S(2)}) collective-permute-start(bf16[576,384]{1,0:T(8,128)(2,1)S(1)} %dynamic-slice_bitcast_fusion.1), channel_id=1, source_target_pairs={{0,4},{2,6},{4,0},{6,2},{8,12},{10,14},{12,8},{14,10},{16,20},{18,... | collective-permute-start | bytes 1327112 | tf_op jit(solution)/shard_map/ppermute | solution.py:247
  12.6 10.5 %collective-permute-done.1 = bf16[576,384]{1,0:T(8,128)(2,1)S(1)} collective-permute-done((bf16[576,384]{1,0:T(8,128)(2,1)S(1)}, bf16[576,384]{1,0:T(8,128)(2,1)S(1)}, u32[]{:S(2)}, u32[]{:S(2)}) %collective-permute-start.1) | collective-permute-done | bytes 442400 | tf_op jit(solution)/shard_map/ppermute | solution.py:247
  23.1 1.9 %collective-permute-start.2 = (bf16[288,384]{1,0:T(8,128)(2,1)S(1)}, bf16[288,384]{1,0:T(8,128)(2,1)S(1)}, u32[]{:S(2)}, u32[]{:S(2)}) collective-permute-start(bf16[288,384]{1,0:T(8,128)(2,1)S(1)} %dynamic-slice_bitcast_fusion.2), channel_id=1, source_target_pairs={{0,8},{2,10},{4,12},{6,14},{8,0},{10,2},{12,4},{14,6},{16,24},{18,... | collective-permute-start | bytes 663560 | tf_op jit(solution)/shard_map/ppermute | solution.py:247
  25.0 5.1 %collective-permute-done.2 = bf16[288,384]{1,0:T(8,128)(2,1)S(1)} collective-permute-done((bf16[288,384]{1,0:T(8,128)(2,1)S(1)}, bf16[288,384]{1,0:T(8,128)(2,1)S(1)}, u32[]{:S(2)}, u32[]{:S(2)}) %collective-permute-start.2) | collective-permute-done | bytes 221216 | tf_op jit(solution)/shard_map/ppermute | solution.py:247
  30.2 2.6 %collective-permute-start.3 = (bf16[144,384]{1,0:T(8,128)(2,1)S(1)}, bf16[144,384]{1,0:T(8,128)(2,1)S(1)}, u32[]{:S(2)}, u32[]{:S(2)}) collective-permute-start(bf16[144,384]{1,0:T(8,128)(2,1)S(1)} %dynamic-slice_bitcast_fusion.3), channel_id=1, source_target_pairs={{0,16},{2,18},{4,20},{6,22},{8,24},{10,26},{12,28},{14,30},{16,0},... | collective-permute-start | bytes 331784 | tf_op jit(solution)/shard_map/ppermute | solution.py:247
  32.8 4.4 %collective-permute-done.3 = bf16[144,384]{1,0:T(8,128)(2,1)S(1)} collective-permute-done((bf16[144,384]{1,0:T(8,128)(2,1)S(1)}, bf16[144,384]{1,0:T(8,128)(2,1)S(1)}, u32[]{:S(2)}, u32[]{:S(2)}) %collective-permute-start.3) | collective-permute-done | bytes 110624 | tf_op jit(solution)/shard_map/ppermute | solution.py:247
  37.2 1.4 collective-permute-start.4
  38.6 4.3 %collective-permute-done.4 = bf16[144,384]{1,0:T(8,128)(2,1)S(1)} collective-permute-done((bf16[144,384]{1,0:T(8,128)(2,1)S(1)}, bf16[144,384]{1,0:T(8,128)(2,1)S(1)}, u32[]{:S(2)}, u32[]{:S(2)}) %collective-permute-start.4) | collective-permute-done | bytes 110624 | tf_op jit(solution)/shard_map/ppermute | solution.py:247
  43.0 3.3 %collective-permute-start.5 = (bf16[288,384]{1,0:T(8,128)(2,1)S(1)}, bf16[288,384]{1,0:T(8,128)(2,1)S(1)}, u32[]{:S(2)}, u32[]{:S(2)}) collective-permute-start(bf16[288,384]{1,0:T(8,128)(2,1)S(1)} %pad_maximum_fusion.5), channel_id=1, source_target_pairs={{0,8},{2,10},{4,12},{6,14},{8,0},{10,2},{12,4},{14,6},{16,24},{18,... | collective-permute-start | bytes 663560 | tf_op jit(solution)/shard_map/ppermute | solution.py:247
  46.3 3.9 %collective-permute-done.5 = bf16[288,384]{1,0:T(8,128)(2,1)S(1)} collective-permute-done((bf16[288,384]{1,0:T(8,128)(2,1)S(1)}, bf16[288,384]{1,0:T(8,128)(2,1)S(1)}, u32[]{:S(2)}, u32[]{:S(2)}) %collective-permute-start.5) | collective-permute-done | bytes 221216 | tf_op jit(solution)/shard_map/ppermute | solution.py:247
  50.2 0.1 broadcast_select_fusion.5
  50.3 1.6 %collective-permute-start.6 = (bf16[576,384]{1,0:T(8,128)(2,1)S(1)}, bf16[576,384]{1,0:T(8,128)(2,1)S(1)}, u32[]{:S(2)}, u32[]{:S(2)}) collective-permute-start(bf16[576,384]{1,0:T(8,128)(2,1)S(1)} %pad_maximum_fusion.4), channel_id=1, source_target_pairs={{0,4},{2,6},{4,0},{6,2},{8,12},{10,14},{12,8},{14,10},{16,20},{18,... | collective-permute-start | bytes 1327112 | tf_op jit(solution)/shard_map/ppermute | solution.py:247
  51.9 0.6 gather_fusion.1
  52.5 0.7 copy.27.nb_ref
  53.2 5.3 %far_pairs.1 = bf16[32,32,128]{2,1,0:T(8,128)(2,1)} custom-call(bf16[4096,128]{1,0:T(8,128)(2,1)} %bitcast.95), custom_call_target="tpu_custom_call" | custom-call | tf_op jit(solution)/shard_map/far_pairs/pallas_call | solution.py:117
  58.4 0.2 collective-permute-done.6
  58.7 0.2 broadcast_select_fusion.3
  58.9 0.1 pad_maximum_fusion.3
  59.0 0.6 broadcast_select_fusion.8.partner_ref
  59.7 24.5 %bounce.1 = bf16[2,16,64,128]{3,2,1,0:T(8,128)(2,1)} custom-call(s32[2,16]{1,0:T(2,128)} %broadcast_select_fusion.8.partner_ref, bf16[16,64,128]{2,1,0:T(8,128)(2,1)} %bitcast.103), custom_call_target="tpu_custom_call" | custom-call | tf_op jit(solution)/shard_map/bounce/pallas_call | solution.py:88
  84.2 1.1 copy.26
  85.3 0.2 fusion.5
  85.6 0.3 maximum_bitcast_fusion
  85.9 1.1 pad_maximum_fusion.2.far_ref
  86.9 10.3 %pair_products.1 = (bf16[16,384,128]{2,1,0:T(8,128)(2,1)}, bf16[16,384,128]{2,1,0:T(8,128)(2,1)}) custom-call(s32[32,2]{1,0:T(8,128)} %copy.27.nb_ref, s32[1]{0:T(128)} %bitcast.half_ref, bf16[2,32,64,128]{3,2,1,0:T(8,128)(2,1)} %pad_maximum_fusion.2.far_ref, bf16[32,128,768]{2,1,0:T(8,128)(2,1)} %bitcast.94, bf16[64,64,128]{2,1,0:T(8,128)(2,1)} %bitcast.96), custom_call_target="tpu_custom_call" | custom-call | flops 1600000000 | bytes 30000000 | tf_op jit(solution)/shard_map/pair_products/pallas_call | solution.py:182
  97.2 1.5 %collective-permute-start.8 = (bf16[16,384,128]{2,1,0:T(8,128)(2,1)}, bf16[16,384,128]{2,1,0:T(8,128)(2,1)}, u32[]{:S(2)}, u32[]{:S(2)}) collective-permute-start(bf16[16,384,128]{2,1,0:T(8,128)(2,1)} %get-tuple-element.8.refs_3_.refs_4_), channel_id=1, source_target_pairs={{0,1},{1,0},{2,3},{3,2},{4,5},{5,4},{6,7},{7,6},{8,9},{9,8},{10,11... | collective-permute-start | bytes 4718600 | tf_op jit(solution)/shard_map/ppermute | solution.py:247
  98.7 0.4 broadcast_select_fusion.1
  99.1 0.9 slice_bitcast_fusion.refs_0_
  100.0 1.2 pad_maximum_fusion.1
  101.1 14.3 %screen_own.1 = f32[128,128]{1,0:T(8,128)} custom-call(bf16[2,768,384]{2,1,0:T(8,128)(2,1)} %bitcast.102, bf16[16,384,128]{2,1,0:T(8,128)(2,1)} %get-tuple-element.7.refs_1_.refs_2_, bf16[16,384,128]{2,1,0:T(8,128)(2,1)} %get-tuple-element.7.refs_1_.refs_2_, bf16[16,384,128]{2,1,0:T(8,128)(2,1)} %get-tuple-element.8.refs_3_.refs_4_, ...), custom_call_target="tpu_custom_call" | custom-call | flops 8000000000 | bytes 20000000 | tf_op jit(solution)/shard_map/screen_own/pallas_call | solution.py:232
  115.5 19.3 %collective-permute-done.8.refs_1_ = bf16[16,384,128]{2,1,0:T(8,128)(2,1)} collective-permute-done((bf16[16,384,128]{2,1,0:T(8,128)(2,1)}, bf16[16,384,128]{2,1,0:T(8,128)(2,1)}, u32[]{:S(2)}, u32[]{:S(2)}) %collective-permute-start.8) | collective-permute-done | bytes 1572896 | tf_op jit(solution)/shard_map/ppermute | solution.py:247
  134.8 8.3 %screen_cross.1 = f32[128,128]{1,0:T(8,128)} custom-call(bf16[1,768,384]{2,1,0:T(8,128)(2,1)} %slice_bitcast_fusion.refs_0_, bf16[16,384,128]{2,1,0:T(8,128)(2,1)} %collective-permute-done.8.refs_1_, bf16[16,384,128]{2,1,0:T(8,128)(2,1)} %get-tuple-element.7.refs_1_.refs_2_), custom_call_target="tpu_custom_call" | custom-call | flops 4000000000 | bytes 10000000 | tf_op jit(solution)/shard_map/screen_cross/pallas_call | solution.py:232
  143.1 0.8 add.125
  144.3 1.5 %collective-permute-start.9 = (f32[32,128]{1,0:T(8,128)S(1)}, f32[32,128]{1,0:T(8,128)S(1)}, u32[]{:S(2)}, u32[]{:S(2)}) collective-permute-start(f32[32,128]{1,0:T(8,128)S(1)} %dynamic-slice_bitcast_fusion.4), channel_id=1, source_target_pairs={{0,1},{1,0},{2,3},{3,2},{4,5},{5,4},{6,7},{7,6},{8,9},{9,8},{10,11... | collective-permute-start | bytes 49160 | tf_op jit(solution)/shard_map/ppermute | solution.py:247
  145.9 2.2 %collective-permute-done.9 = f32[32,128]{1,0:T(8,128)S(1)} collective-permute-done((f32[32,128]{1,0:T(8,128)S(1)}, f32[32,128]{1,0:T(8,128)S(1)}, u32[]{:S(2)}, u32[]{:S(2)}) %collective-permute-start.9) | collective-permute-done | bytes 16416 | tf_op jit(solution)/shard_map/ppermute | solution.py:247
  148.1 0.6 fusion.3
  (25 shorter events, 0.8 us)
Async XLA Ops:
  0.0 51.9 %copy-start = (s32[2,16]{1,0:T(2,128)S(1)}, s32[2,16]{1,0:T(2,128)}, u32[]{:S(2)}) copy-start(s32[2,16]{1,0:T(2,128)} %param.10) | copy-start | bytes 388
  6.8 2.6 %collective-permute-start = (bf16[1152,384]{1,0:T(8,128)(2,1)S(1)}, bf16[1152,384]{1,0:T(8,128)(2,1)S(1)}, u32[]{:S(2)}, u32[]{:S(2)}) collective-permute-start(bf16[1152,384]{1,0:T(8,128)(2,1)S(1)} %dynamic-slice_bitcast_fusion), channel_id=1, source_target_pairs={{0,2},{2,0},{4,6},{6,4},{8,10},{10,8},{12,14},{14,12},{16,18},{18,... | collective-permute-start | bytes 2654216 | tf_op jit(solution)/shard_map/ppermute | solution.py:247
  9.6 13.4 %collective-permute-start.1 = (bf16[576,384]{1,0:T(8,128)(2,1)S(1)}, bf16[576,384]{1,0:T(8,128)(2,1)S(1)}, u32[]{:S(2)}, u32[]{:S(2)}) collective-permute-start(bf16[576,384]{1,0:T(8,128)(2,1)S(1)} %dynamic-slice_bitcast_fusion.1), channel_id=1, source_target_pairs={{0,4},{2,6},{4,0},{6,2},{8,12},{10,14},{12,8},{14,10},{16,20},{18,... | collective-permute-start | bytes 1327112 | tf_op jit(solution)/shard_map/ppermute | solution.py:247
  23.1 7.0 %collective-permute-start.2 = (bf16[288,384]{1,0:T(8,128)(2,1)S(1)}, bf16[288,384]{1,0:T(8,128)(2,1)S(1)}, u32[]{:S(2)}, u32[]{:S(2)}) collective-permute-start(bf16[288,384]{1,0:T(8,128)(2,1)S(1)} %dynamic-slice_bitcast_fusion.2), channel_id=1, source_target_pairs={{0,8},{2,10},{4,12},{6,14},{8,0},{10,2},{12,4},{14,6},{16,24},{18,... | collective-permute-start | bytes 663560 | tf_op jit(solution)/shard_map/ppermute | solution.py:247
  30.1 22.3 %copy-start.2 = (s32[32,2]{0,1:T(2,128)S(1)}, s32[32,2]{0,1:T(2,128)}, u32[]{:S(2)}) copy-start(s32[32,2]{0,1:T(2,128)} %param.8) | copy-start | bytes 772
  30.2 7.0 %collective-permute-start.3 = (bf16[144,384]{1,0:T(8,128)(2,1)S(1)}, bf16[144,384]{1,0:T(8,128)(2,1)S(1)}, u32[]{:S(2)}, u32[]{:S(2)}) collective-permute-start(bf16[144,384]{1,0:T(8,128)(2,1)S(1)} %dynamic-slice_bitcast_fusion.3), channel_id=1, source_target_pairs={{0,16},{2,18},{4,20},{6,22},{8,24},{10,26},{12,28},{14,30},{16,0},... | collective-permute-start | bytes 331784 | tf_op jit(solution)/shard_map/ppermute | solution.py:247
  37.2 5.7 %collective-permute-start.4 = (bf16[144,384]{1,0:T(8,128)(2,1)S(1)}, bf16[144,384]{1,0:T(8,128)(2,1)S(1)}, u32[]{:S(2)}, u32[]{:S(2)}) collective-permute-start(bf16[144,384]{1,0:T(8,128)(2,1)S(1)} %bitcast_add_fusion.3), channel_id=1, source_target_pairs={{0,16},{2,18},{4,20},{6,22},{8,24},{10,26},{12,28},{14,30},{16,0},... | collective-permute-start | bytes 331784 | tf_op jit(solution)/shard_map/ppermute | solution.py:247
  43.0 7.2 %collective-permute-start.5 = (bf16[288,384]{1,0:T(8,128)(2,1)S(1)}, bf16[288,384]{1,0:T(8,128)(2,1)S(1)}, u32[]{:S(2)}, u32[]{:S(2)}) collective-permute-start(bf16[288,384]{1,0:T(8,128)(2,1)S(1)} %pad_maximum_fusion.5), channel_id=1, source_target_pairs={{0,8},{2,10},{4,12},{6,14},{8,0},{10,2},{12,4},{14,6},{16,24},{18,... | collective-permute-start | bytes 663560 | tf_op jit(solution)/shard_map/ppermute | solution.py:247
  50.3 8.4 %collective-permute-start.6 = (bf16[576,384]{1,0:T(8,128)(2,1)S(1)}, bf16[576,384]{1,0:T(8,128)(2,1)S(1)}, u32[]{:S(2)}, u32[]{:S(2)}) collective-permute-start(bf16[576,384]{1,0:T(8,128)(2,1)S(1)} %pad_maximum_fusion.4), channel_id=1, source_target_pairs={{0,4},{2,6},{4,0},{6,2},{8,12},{10,14},{12,8},{14,10},{16,20},{18,... | collective-permute-start | bytes 1327112 | tf_op jit(solution)/shard_map/ppermute | solution.py:247
  59.0 39.8 %collective-permute-start.7 = (bf16[1152,384]{1,0:T(8,128)(2,1)S(1)}, bf16[1152,384]{1,0:T(8,128)(2,1)S(1)}, u32[]{:S(2)}, u32[]{:S(2)}) collective-permute-start(bf16[1152,384]{1,0:T(8,128)(2,1)S(1)} %pad_maximum_fusion.3), channel_id=1, source_target_pairs={{0,2},{2,0},{4,6},{6,4},{8,10},{10,8},{12,14},{14,12},{16,18},{18,... | collective-permute-start | bytes 2654216 | tf_op jit(solution)/shard_map/ppermute | solution.py:247
  97.2 37.6 %collective-permute-start.8 = (bf16[16,384,128]{2,1,0:T(8,128)(2,1)}, bf16[16,384,128]{2,1,0:T(8,128)(2,1)}, u32[]{:S(2)}, u32[]{:S(2)}) collective-permute-start(bf16[16,384,128]{2,1,0:T(8,128)(2,1)} %get-tuple-element.8.refs_3_.refs_4_), channel_id=1, source_target_pairs={{0,1},{1,0},{2,3},{3,2},{4,5},{5,4},{6,7},{7,6},{8,9},{9,8},{10,11... | collective-permute-start | bytes 4718600 | tf_op jit(solution)/shard_map/ppermute | solution.py:247
  115.5 27.6 %copy-start.1 = (f32[128,128]{1,0:T(8,128)S(1)}, f32[128,128]{1,0:T(8,128)}, u32[]{:S(2)}) copy-start(f32[128,128]{1,0:T(8,128)} %screen_own.1) | copy-start | bytes 196612
  144.3 3.8 %collective-permute-start.9 = (f32[32,128]{1,0:T(8,128)S(1)}, f32[32,128]{1,0:T(8,128)S(1)}, u32[]{:S(2)}, u32[]{:S(2)}) collective-permute-start(f32[32,128]{1,0:T(8,128)S(1)} %dynamic-slice_bitcast_fusion.4), channel_id=1, source_target_pairs={{0,1},{1,0},{2,3},{3,2},{4,5},{5,4},{6,7},{7,6},{8,9},{9,8},{10,11... | collective-permute-start | bytes 49160 | tf_op jit(solution)/shard_map/ppermute | solution.py:247
